TPU v7x, 256 devices: a whole 4x4x8 slice. The times are simulated.
256 devices in a mesh: rows: 64 (over z, x, core), cols: 4 (over y).
Axes of the slice: x: 4, y: 4, z: 8, core: 2. Of those that a mesh axis runs over, the one named last changes fastest.
Arguments:
- embeddings: bfloat16 [65536, 512], P('rows'), may hold values from -90 to 90
- neighbours: int32 [256, 12], P('rows'), may hold values from -1 to 255, as said below
- queries: float32 [65536, 512], P('rows', 'cols'), may hold values from -22 to 22
Outputs:
- diffused: float32 [65536, 512], P('rows', 'cols')
Inputs may be any that keep to these rules, and one draw needn't show every extreme that they name: `neighbours`: row b lists in rising order the distinct blocks linked to block b, then -1 in the remaining slots. Every block is linked to itself, links are symmetric, and a linked block lies on the same index of rows as b or on an adjacent one, block c lying on index c // 4. Some block has 12 links.
All inputs are finite; a program needn't handle non-finite values.
Results may differ from a plain program's by a relative error of at most 0.00039.
Values may be sent and summed in bfloat16 or wider, within the bound.
No kernel may reach another device: no remote copies, remote signals or barrier semaphores. Data moves between devices by JAX's collectives and lax.ppermute only.
A program may use at most 128 MiB of HBM per device.

v0:
```python
import jax
import jax.numpy as jnp
from jax import lax
from jax.sharding import PartitionSpec as P

ITERS = 3
diffusion = 0.9
epsilon = 1e-06
highest = lax.Precision.HIGHEST
contract_rows = (((1,), (1,)), ((), ()))


def extended(array, sides, width):
    for axis, dim in sides:
        peers, length = (lax.axis_size(axis), array.shape[dim])
        up = [(i, (i + 1) % peers) for i in range(peers - 1)]
        down = [(j, i) for i, j in up]
        last = lax.slice_in_dim(array, length - width, length, axis=dim)
        leading = lax.slice_in_dim(array, 0, width, axis=dim)
        before = lax.ppermute(last, axis, up)
        after = lax.ppermute(leading, axis, down)
        array = jnp.concatenate([before, array, after], axis=dim)
    return array


def column_sums(left_side, right_side):
    return jnp.sum(left_side * right_side, axis=0)


def squares(residual):
    return lax.psum(column_sums(residual, residual), "rows")


def shards(embeddings, neighbours, queries):
    own_blocks = neighbours.shape[0]
    own_rows = embeddings.shape[0]
    block_rows = own_rows // own_blocks
    features = embeddings.shape[1]
    values = embeddings.astype(jnp.float32)
    normed = (values * lax.rsqrt(jnp.sum(values * values, axis=1, keepdims=True) + epsilon)).astype(
        jnp.bfloat16
    )
    stacked = normed.reshape(own_blocks, block_rows, features)
    beside_all = extended(stacked, (("rows", 0),), own_blocks)
    similar = lax.dot_general(
        normed,
        beside_all.reshape(3 * own_rows, features),
        contract_rows,
        preferred_element_type=jnp.float32,
    )
    lowest = (lax.axis_index("rows") - 1) * own_blocks
    candidates = lowest + jnp.arange(3 * own_blocks, dtype=jnp.int32)
    linked = jnp.any(neighbours[:, :, None] == candidates[None, None, :], axis=1).astype(
        jnp.float32
    )
    cubed = jnp.maximum(similar, 0.0) ** 3
    affinity = (
        cubed.reshape(own_blocks, block_rows, 3 * own_blocks, block_rows) * linked[:, None, :, None]
    ).reshape(own_rows, 3 * own_rows)
    inv_root = lax.rsqrt(jnp.sum(affinity, axis=1))
    far_roots = extended(inv_root.reshape(own_blocks, block_rows), (("rows", 0),), own_blocks)
    banded = affinity * inv_root[:, None] * far_roots.reshape(1, 3 * own_rows)
    solution = jnp.zeros_like(queries)
    residual = queries
    direction = queries
    residual_sq = squares(residual)
    for iteration in range(ITERS):
        columns = direction.shape[1]
        outgoing = direction
        nearby = extended(
            outgoing.reshape(own_blocks, block_rows, columns), (("rows", 0),), own_blocks
        )
        mixed = jnp.dot(
            banded,
            nearby.reshape(3 * own_rows, columns),
            precision=highest,
            preferred_element_type=jnp.float32,
        )
        image = direction - diffusion * mixed
        curvature = lax.psum(column_sums(direction, image), "rows")
        step_size = residual_sq / curvature
        solution = solution + step_size * direction
        residual = residual - step_size * image
        if iteration + 1 < ITERS:
            updated = squares(residual)
            direction = residual + updated / residual_sq * direction
            residual_sq = updated
    return solution


def solution(mesh):
    placed = (P("rows", None), P("rows", None), P("rows", "cols"))
    return jax.shard_map(
        shards, mesh=mesh, in_specs=placed, out_specs=P("rows", "cols"), check_vma=False
    )
```

profile of v0, /device:TPU:145, one launch (start us, length us, event | category | flops | bytes accessed | tf_op | source)
XLA Modules:
  0.0 768.8 jit_solution(9624634156711667488)
XLA Ops:
  0.0 1.6 fusion.10
  1.6 1.5 fusion.11
  3.1 2.6 collective-permute-start.1
  5.7 3.0 collective-permute-start
  8.7 0.0 copy-done
  8.7 2.6 collective-permute-start.5
  11.3 3.0 collective-permute-start.4
  14.3 0.0 copy-done.1
  14.3 0.1 copy.5
  14.4 0.1 compare_reduce_fusion
  14.5 0.1 copy.6
  14.6 6.2 mul.127
  20.8 12.3 %copy.8 = f32[384,8,4,256]{3,1,2,0:T(8,128)} copy(f32[384,8,4,256]{3,2,1,0:T(4,128)} %bitcast.18) | data formatting | bytes 25165824
  33.1 12.6 %copy.7 = f32[1024,3072]{1,0:T(8,128)} copy(f32[1024,3072]{0,1:T(8,128)} %bitcast.19) | data formatting | bytes 25165824 | tf_op jit(solution)/shard_map/mul | solution.py:58
  45.7 0.0 collective-permute-done.1
  45.7 0.0 collective-permute-done
  45.7 1.4 pad_maximum_fusion
  47.1 9.5 %fusion.20 = (f32[1024]{0:T(1024)S(1)}, f32[1024,3072]{1,0:T(8,128)}) fusion(f32[1024,3072]{1,0:T(8,128)} %copy.7, bf16[1024,512]{1,0:T(8,128)(2,1)S(1)} %fusion.11, bf16[3072,512]{1,0:T(8,128)(2,1)S(1)} %bitcast.29), kind=kOutput, calls=%fused_computation.42 | convolution fusion | flops 3236953088 | bytes 29364224 | tf_op jit(solution)/shard_map/dot_general | solution.py:45
  56.6 5.9 collective-permute-start.3
  62.5 2.1 collective-permute-start.2
  64.6 0.0 collective-permute-done.5
  64.6 0.0 collective-permute-done.4
  64.6 1.1 pad_maximum_fusion.1
  65.8 0.0 collective-permute-done.3
  65.8 4.3 collective-permute-done.2
  70.2 13.3 %multiply_reduce_fusion.3 = (f32[128]{0:T(128)S(1)}, f32[128]{0:T(128)S(1)}, f32[1024,128]{1,0:T(8,128)S(1)}) fusion(f32[1024,128]{1,0:T(8,128)S(1)} %copy-done, f32[3072,128]{1,0:T(8,128)S(1)} %bitcast.33, f32[1024,3072]{1,0:T(8,128)} %get-tuple-element.12, f32[3072]{0:T(1024)S(1)} %mul.132, f32[1024]{0:T(1024)S(1)} %rsqrt.20), kind=kOutput, calls=%fused_computation.36 | convolution fusion | flops 4838916096 | bytes 15221760 | tf_op jit(solution)/shard_map/dot_general | solution.py:73
  83.5 129.1 %all-reduce = (f32[128]{0:T(128)S(1)}, f32[128]{0:T(128)S(1)}) all-reduce(f32[128]{0:T(128)S(1)} %get-tuple-element.6, f32[128]{0:T(128)S(1)} %get-tuple-element.5), channel_id=1, replica_groups=mesh['rows'=64,'cols'=4] {'rows'}, use_global_device_ids=true, to_apply=%region_1.0 | all-reduce | flops 256 | bytes 2048 | tf_op jit(solution)/shard_map/psum | solution.py:31
  212.6 0.2 multiply_reduce_fusion.2
  212.7 124.1 %psum.44 = f32[128]{0:T(128)S(1)} all-reduce(f32[128]{0:T(128)S(1)} %get-tuple-element.9), channel_id=1, replica_groups=mesh['rows'=64,'cols'=4] {'rows'}, use_global_device_ids=true, to_apply=%region_8.0 | all-reduce | flops 128 | bytes 1024 | tf_op jit(solution)/shard_map/psum | solution.py:31
  336.9 0.1 multiply_add_fusion.2
  336.9 2.6 collective-permute-start.7
  339.5 3.0 collective-permute-start.6
  342.5 5.2 collective-permute-done.7
  347.7 0.9 collective-permute-done.6
  348.6 0.1 pad_maximum_fusion.2
  348.7 13.3 %multiply_reduce_fusion.1 = (f32[128]{0:T(128)S(1)}, f32[1024,128]{1,0:T(8,128)S(1)}) fusion(f32[1024,128]{1,0:T(8,128)S(1)} %multiply_add_fusion.2, f32[3072,128]{1,0:T(8,128)S(1)} %bitcast.35, f32[1024,3072]{1,0:T(8,128)} %get-tuple-element.12, f32[3072]{0:T(1024)S(1)} %mul.132, f32[1024]{0:T(1024)S(1)} %rsqrt.20), kind=kOutput, calls=%fused_computation.32 | convolution fusion | flops 4838653952 | bytes 15221248 | tf_op jit(solution)/shard_map/dot_general | solution.py:73
  362.1 128.3 %psum.45 = f32[128]{0:T(128)S(1)} all-reduce(f32[128]{0:T(128)S(1)} %get-tuple-element.14), channel_id=1, replica_groups=mesh['rows'=64,'cols'=4] {'rows'}, use_global_device_ids=true, to_apply=%region_10.0 | all-reduce | flops 128 | bytes 1024 | tf_op jit(solution)/shard_map/psum | solution.py:80
  490.4 0.2 multiply_reduce_fusion
  490.6 124.1 %psum.46 = f32[128]{0:T(128)S(1)} all-reduce(f32[128]{0:T(128)S(1)} %multiply_reduce_fusion), channel_id=1, replica_groups=mesh['rows'=64,'cols'=4] {'rows'}, use_global_device_ids=true, to_apply=%region_12.0 | all-reduce | flops 128 | bytes 1024 | tf_op jit(solution)/shard_map/psum | solution.py:31
  614.7 0.1 multiply_add_fusion.1
  614.7 2.6 collective-permute-start.9
  617.3 3.0 collective-permute-start.8
  620.3 5.2 collective-permute-done.9
  625.5 0.9 collective-permute-done.8
  626.4 0.1 pad_maximum_fusion.3
  626.5 13.2 %fusion.19 = f32[128]{0:T(128)S(1)} fusion(f32[1024,128]{1,0:T(8,128)S(1)} %multiply_add_fusion.1, f32[3072,128]{1,0:T(8,128)S(1)} %bitcast.34, f32[1024,3072]{1,0:T(8,128)} %get-tuple-element.12, f32[3072]{0:T(1024)S(1)} %mul.132, f32[1024]{0:T(1024)S(1)} %rsqrt.20), kind=kOutput, calls=%fused_computation.27 | convolution fusion | flops 4838653952 | bytes 14696960 | tf_op jit(solution)/shard_map/dot_general | solution.py:73
  639.8 128.1 %psum.47 = f32[128]{0:T(128)S(1)} all-reduce(f32[128]{0:T(128)S(1)} %fusion.19), channel_id=1, replica_groups=mesh['rows'=64,'cols'=4] {'rows'}, use_global_device_ids=true, to_apply=%region_14.0 | all-reduce | flops 128 | bytes 1024 | tf_op jit(solution)/shard_map/psum | solution.py:80
  767.9 0.9 multiply_add_fusion
  (14 shorter events, 0.1 us)
Async XLA Ops:
  0.0 8.7 %copy-start = (f32[1024,128]{1,0:T(8,128)S(1)}, f32[1024,128]{1,0:T(8,128)}, u32[]{:S(2)}) copy-start(f32[1024,128]{1,0:T(8,128)} %param.5) | copy-start | bytes 1572868
  0.0 14.3 %copy-start.1 = (s32[4,12]{1,0:T(4,128)S(1)}, s32[4,12]{1,0:T(4,128)}, u32[]{:S(2)}) copy-start(s32[4,12]{1,0:T(4,128)} %param.4) | copy-start | bytes 580
  3.1 42.6 %collective-permute-start.1 = (bf16[4,256,512]{2,1,0:T(8,128)(2,1)S(1)}, bf16[4,256,512]{2,1,0:T(8,128)(2,1)S(1)}, u32[]{:S(2)}, u32[]{:S(2)}) collective-permute-start(bf16[4,256,512]{2,1,0:T(8,128)(2,1)S(1)} %bitcast.26), channel_id=1, source_target_pairs={{4,0},{8,4},{12,8},{16,12},{20,16},{24,20},{28,24},{32,28},{36,32}... | collective-permute-start | bytes 3145736 | tf_op jit(solution)/shard_map/ppermute | solution.py:21
  5.7 40.0 %collective-permute-start = (bf16[4,256,512]{2,1,0:T(8,128)(2,1)S(1)}, bf16[4,256,512]{2,1,0:T(8,128)(2,1)}, u32[]{:S(2)}, u32[]{:S(2)}) collective-permute-start(bf16[4,256,512]{2,1,0:T(8,128)(2,1)S(1)} %bitcast.27), channel_id=1, source_target_pairs={{0,4},{4,8},{8,12},{12,16},{16,20},{20,24},{24,28},{28,32},{32,36}... | collective-permute-start | bytes 3145736 | tf_op jit(solution)/shard_map/ppermute | solution.py:20
  8.7 55.9 %collective-permute-start.5 = (f32[4,256,128]{2,1,0:T(8,128)S(1)}, f32[4,256,128]{2,1,0:T(8,128)S(1)}, u32[]{:S(2)}, u32[]{:S(2)}) collective-permute-start(f32[4,256,128]{2,1,0:T(8,128)S(1)} %bitcast.20), channel_id=1, source_target_pairs={{4,0},{8,4},{12,8},{16,12},{20,16},{24,20},{28,24},{32,28},{36,32}... | collective-permute-start | bytes 1572872 | tf_op jit(solution)/shard_map/ppermute | solution.py:21
  11.3 53.4 %collective-permute-start.4 = (f32[4,256,128]{2,1,0:T(8,128)S(1)}, f32[4,256,128]{2,1,0:T(8,128)}, u32[]{:S(2)}, u32[]{:S(2)}) collective-permute-start(f32[4,256,128]{2,1,0:T(8,128)S(1)} %bitcast.21), channel_id=1, source_target_pairs={{0,4},{4,8},{8,12},{12,16},{16,20},{20,24},{24,28},{28,32},{32,36}... | collective-permute-start | bytes 1572872 | tf_op jit(solution)/shard_map/ppermute | solution.py:20
  56.6 9.2 %collective-permute-start.3 = (f32[4,256]{1,0:T(4,128)S(1)}, f32[4,256]{1,0:T(4,128)S(1)}, u32[]{:S(2)}, u32[]{:S(2)}) collective-permute-start(f32[4,256]{1,0:T(4,128)S(1)} %rsqrt.21), channel_id=1, source_target_pairs={{4,0},{8,4},{12,8},{16,12},{20,16},{24,20},{28,24},{32,28},{36,32}... | collective-permute-start | bytes 12296 | tf_op jit(solution)/shard_map/ppermute | solution.py:21
  62.5 7.6 collective-permute-start.2
  336.9 10.8 %collective-permute-start.7 = (f32[4,256,128]{2,1,0:T(8,128)S(1)}, f32[4,256,128]{2,1,0:T(8,128)S(1)}, u32[]{:S(2)}, u32[]{:S(2)}) collective-permute-start(f32[4,256,128]{2,1,0:T(8,128)S(1)} %bitcast.23), channel_id=1, source_target_pairs={{4,0},{8,4},{12,8},{16,12},{20,16},{24,20},{28,24},{32,28},{36,32}... | collective-permute-start | bytes 1572872 | tf_op jit(solution)/shard_map/ppermute | solution.py:21
  339.5 9.1 %collective-permute-start.6 = (f32[4,256,128]{2,1,0:T(8,128)S(1)}, f32[4,256,128]{2,1,0:T(8,128)S(1)}, u32[]{:S(2)}, u32[]{:S(2)}) collective-permute-start(f32[4,256,128]{2,1,0:T(8,128)S(1)} %bitcast.24), channel_id=1, source_target_pairs={{0,4},{4,8},{8,12},{12,16},{16,20},{20,24},{24,28},{28,32},{32,36}... | collective-permute-start | bytes 1572872 | tf_op jit(solution)/shard_map/ppermute | solution.py:20
  614.7 10.8 %collective-permute-start.9 = (f32[4,256,128]{2,1,0:T(8,128)S(1)}, f32[4,256,128]{2,1,0:T(8,128)S(1)}, u32[]{:S(2)}, u32[]{:S(2)}) collective-permute-start(f32[4,256,128]{2,1,0:T(8,128)S(1)} %bitcast.30), channel_id=1, source_target_pairs={{4,0},{8,4},{12,8},{16,12},{20,16},{24,20},{28,24},{32,28},{36,32}... | collective-permute-start | bytes 1572872 | tf_op jit(solution)/shard_map/ppermute | solution.py:21
  617.3 9.1 %collective-permute-start.8 = (f32[4,256,128]{2,1,0:T(8,128)S(1)}, f32[4,256,128]{2,1,0:T(8,128)S(1)}, u32[]{:S(2)}, u32[]{:S(2)}) collective-permute-start(f32[4,256,128]{2,1,0:T(8,128)S(1)} %bitcast.31), channel_id=1, source_target_pairs={{0,4},{4,8},{8,12},{12,16},{16,20},{20,24},{24,28},{28,32},{32,36}... | collective-permute-start | bytes 1572872 | tf_op jit(solution)/shard_map/ppermute | solution.py:20
where the time goes:
time: 770 us; the launch traced here: 769 us
  blocking collectives  634 us (82%)
  matrix products  49.4 us (6%)
  local copies, waits for them, and re-layouts  31.3 us (4%)
  starting transfers between devices  30.3 us (4%)
  waiting for transfers between devices  16.5 us (2%)
    psum x3, blocking collectives, squares(): return lax.psum(column_sums(residual, residual), 'rows')  377 us
    psum x2, blocking collectives, shards(): curvature = lax.psum(column_sums(direction, image), 'rows')  256 us
    dot_general x3, matrix products, shards(): jnp.dot(banded, nearby.reshape(3 * own_rows, columns), precision=highest,...  39.9 us
    mul x2, local copies, waits for them, and re-layouts, shards(): cubed.reshape(own_blocks, block_rows, 3 * own_blocks, block_rows)  18.8 us
    ppermute x5, starting transfers between devices, extended(): after = lax.ppermute(leading, axis, down)  16.1 us
  transfers between devices with their start and end apart: 10, of which 5 were waited for; matrix products, arithmetic and copies ran while one was open for 6% of the time, Pallas kernels for 0%

commit v1 on v0

--- a/solution.py
+++ b/solution.py
@@ -77,7 +77,9 @@
             preferred_element_type=jnp.float32,
         )
         image = direction - diffusion * mixed
-        curvature = lax.psum(column_sums(direction, image), "rows")
+        own = column_sums(direction, image)
+        pieces = lax.all_gather(own, "rows", axis=0, tiled=False)
+        curvature = pieces.sum(axis=0)
         step_size = residual_sq / curvature
         solution = solution + step_size * direction
         residual = residual - step_size * image

time: 770 us -> 638 us (0.83)
  blocking collectives: 634 us -> 494 us
    psum x2 -> x0, blocking collectives: 256 us -> none  [shards(): curvature = lax.psum(column_sums(direction, image), 'rows')]
    all_gather x0 -> x3, blocking collectives: none -> 118 us  [shards(): pieces = lax.all_gather(own, 'rows', axis=0, tiled=False)]
  transfers between devices with their start and end apart: 10 -> 10, of which waited for: 5 -> 5; matrix products, arithmetic and copies ran while one was open for 6% -> 7% of each run, Pallas kernels for 0% -> 0%
where the time goes in v1:
time: 638 us; the launch traced here: 632 us
  blocking collectives  494 us (77%)
  matrix products  49.4 us (8%)
  starting transfers between devices  33.3 us (5%)
  local copies, waits for them, and re-layouts  31.3 us (5%)
  waiting for transfers between devices  16.1 us (3%)
  other arithmetic  7.59 us (1%)
    psum x3, blocking collectives, squares(): return lax.psum(column_sums(residual, residual), 'rows')  376 us
    all_gather x3, blocking collectives, shards(): pieces = lax.all_gather(own, 'rows', axis=0, tiled=False)  118 us
    dot_general x3, matrix products, shards(): jnp.dot(banded, nearby.reshape(3 * own_rows, columns), precision=highest,...  39.9 us
    ppermute x5, starting transfers between devices, extended(): after = lax.ppermute(leading, axis, down)  20.8 us
    mul x2, local copies, waits for them, and re-layouts, shards(): cubed.reshape(own_blocks, block_rows, 3 * own_blocks, block_rows)  18.8 us
  transfers between devices with their start and end apart: 10, of which 5 were waited for; matrix products, arithmetic and copies ran while one was open for 7% of the time, Pallas kernels for 0%

profile of v1, /device:TPU:145, one launch (start us, length us, event | category | flops | bytes accessed | tf_op | source)
XLA Modules:
  0.0 632.1 jit_solution(8565947439064509636)
XLA Ops:
  0.0 1.6 fusion.10
  1.6 1.5 fusion.11
  3.1 2.6 collective-permute-start.1
  5.7 3.0 collective-permute-start
  8.7 2.6 collective-permute-start.5
  11.3 3.0 collective-permute-start.4
  14.3 0.1 copy.6
  14.4 0.1 compare_reduce_fusion
  14.5 0.1 copy.7
  14.6 6.2 mul.127
  20.8 12.3 %copy.9 = f32[384,8,4,256]{3,1,2,0:T(8,128)} copy(f32[384,8,4,256]{3,2,1,0:T(4,128)} %bitcast.21) | data formatting | bytes 25165824
  33.1 12.6 %copy.8 = f32[1024,3072]{1,0:T(8,128)} copy(f32[1024,3072]{0,1:T(8,128)} %bitcast.22) | data formatting | bytes 25165824 | tf_op jit(solution)/shard_map/mul | solution.py:58
  45.7 0.0 collective-permute-done.1
  45.7 0.0 collective-permute-done
  45.7 1.4 pad_maximum_fusion
  47.1 9.5 %fusion.20 = (f32[1024]{0:T(1024)S(1)}, f32[1024,3072]{1,0:T(8,128)}) fusion(f32[1024,3072]{1,0:T(8,128)} %copy.8, bf16[1024,512]{1,0:T(8,128)(2,1)S(1)} %fusion.11, bf16[3072,512]{1,0:T(8,128)(2,1)S(1)} %bitcast.32), kind=kOutput, calls=%fused_computation.42 | convolution fusion | flops 3236953088 | bytes 29364224 | tf_op jit(solution)/shard_map/dot_general | solution.py:45
  56.6 5.9 collective-permute-start.3
  62.5 2.1 collective-permute-start.2
  64.6 0.0 collective-permute-done.4
  64.6 1.1 pad_maximum_fusion.1
  65.8 4.3 collective-permute-done.2
  70.2 13.3 %multiply_reduce_fusion.3 = (f32[128]{0:T(128)S(1)}, f32[128]{0:T(128)S(1)}, f32[1024,128]{1,0:T(8,128)S(1)}) fusion(f32[1024,128]{1,0:T(8,128)S(1)} %copy-done, f32[3072,128]{1,0:T(8,128)S(1)} %bitcast.36, f32[1024,3072]{1,0:T(8,128)} %get-tuple-element.10, f32[3072]{0:T(1024)S(1)} %mul.132, f32[1024]{0:T(1024)S(1)} %rsqrt.20), kind=kOutput, calls=%fused_computation.36 | convolution fusion | flops 4838916096 | bytes 15221760 | tf_op jit(solution)/shard_map/dot_general | solution.py:73
  83.5 129.1 %psum.21 = f32[128]{0:T(128)S(1)} all-reduce(f32[128]{0:T(128)S(1)} %get-tuple-element.6), channel_id=1, replica_groups=mesh['rows'=64,'cols'=4] {'rows'}, use_global_device_ids=true, to_apply=%region_1.0 | all-reduce | flops 128 | bytes 1024 | tf_op jit(solution)/shard_map/psum | solution.py:31
  212.6 36.0 %all-gather.3 = f32[64,1,128]{2,1,0:T(1,128)S(1)} all-gather(f32[1,1,128]{2,1,0:T(1,128)S(1)} %bitcast.39), channel_id=2, replica_groups=mesh['rows'=64,'cols'=4] {'rows'}, dimensions={0}, use_global_device_ids=true | all-gather | bytes 33280 | tf_op jit(solution)/shard_map/all_gather | solution.py:81
  248.5 0.1 reduce_sum.103
  248.6 0.2 multiply_reduce_fusion.2
  248.8 123.6 %psum.22 = f32[128]{0:T(128)S(1)} all-reduce(f32[128]{0:T(128)S(1)} %get-tuple-element.7), channel_id=1, replica_groups=mesh['rows'=64,'cols'=4] {'rows'}, use_global_device_ids=true, to_apply=%region_8.0 | all-reduce | flops 128 | bytes 1024 | tf_op jit(solution)/shard_map/psum | solution.py:31
  372.3 0.1 multiply_add_fusion.2
  372.4 4.9 collective-permute-start.7
  377.3 2.1 collective-permute-start.6
  379.5 3.4 collective-permute-done.7
  382.9 2.5 collective-permute-done.6
  385.4 0.1 pad_maximum_fusion.2
  385.5 13.3 %multiply_reduce_fusion.1 = (f32[128]{0:T(128)S(1)}, f32[1024,128]{1,0:T(8,128)S(1)}) fusion(f32[1024,128]{1,0:T(8,128)S(1)} %multiply_add_fusion.2, f32[3072,128]{1,0:T(8,128)S(1)} %bitcast.38, f32[1024,3072]{1,0:T(8,128)} %get-tuple-element.10, f32[3072]{0:T(1024)S(1)} %mul.132, f32[1024]{0:T(1024)S(1)} %rsqrt.20), kind=kOutput, calls=%fused_computation.32 | convolution fusion | flops 4838653952 | bytes 15221248 | tf_op jit(solution)/shard_map/dot_general | solution.py:73
  398.8 41.0 %all-gather.4 = f32[64,1,128]{2,1,0:T(1,128)S(1)} all-gather(f32[1,1,128]{2,1,0:T(1,128)S(1)} %bitcast.41), channel_id=3, replica_groups=mesh['rows'=64,'cols'=4] {'rows'}, dimensions={0}, use_global_device_ids=true | all-gather | bytes 33280 | tf_op jit(solution)/shard_map/all_gather | solution.py:81
  439.9 0.1 reduce_sum.106
  439.9 0.2 multiply_reduce_fusion
  440.1 123.6 %psum.23 = f32[128]{0:T(128)S(1)} all-reduce(f32[128]{0:T(128)S(1)} %multiply_reduce_fusion), channel_id=1, replica_groups=mesh['rows'=64,'cols'=4] {'rows'}, use_global_device_ids=true, to_apply=%region_12.0 | all-reduce | flops 128 | bytes 1024 | tf_op jit(solution)/shard_map/psum | solution.py:31
  563.7 0.1 multiply_add_fusion.1
  563.8 4.9 collective-permute-start.9
  568.7 2.2 collective-permute-start.8
  570.9 3.4 collective-permute-done.9
  574.3 2.5 collective-permute-done.8
  576.7 0.1 pad_maximum_fusion.3
  576.8 13.2 %fusion.19 = f32[128]{0:T(128)S(1)} fusion(f32[1024,128]{1,0:T(8,128)S(1)} %multiply_add_fusion.1, f32[3072,128]{1,0:T(8,128)S(1)} %bitcast.37, f32[1024,3072]{1,0:T(8,128)} %get-tuple-element.10, f32[3072]{0:T(1024)S(1)} %mul.132, f32[1024]{0:T(1024)S(1)} %rsqrt.20), kind=kOutput, calls=%fused_computation.27 | convolution fusion | flops 4838653952 | bytes 14696960 | tf_op jit(solution)/shard_map/dot_general | solution.py:73
  590.1 41.0 %all-gather.5 = f32[64,1,128]{2,1,0:T(1,128)S(1)} all-gather(f32[1,1,128]{2,1,0:T(1,128)S(1)} %bitcast.40), channel_id=4, replica_groups=mesh['rows'=64,'cols'=4] {'rows'}, dimensions={0}, use_global_device_ids=true | all-gather | bytes 33280 | tf_op jit(solution)/shard_map/all_gather | solution.py:81
  631.1 0.1 reduce_sum.109
  631.2 0.9 multiply_add_fusion
  (18 shorter events, 0.1 us)
Async XLA Ops:
  0.0 8.7 %copy-start = (f32[1024,128]{1,0:T(8,128)S(1)}, f32[1024,128]{1,0:T(8,128)}, u32[]{:S(2)}) copy-start(f32[1024,128]{1,0:T(8,128)} %param.5) | copy-start | bytes 1572868
  0.0 14.3 %copy-start.1 = (s32[4,12]{1,0:T(4,128)S(1)}, s32[4,12]{1,0:T(4,128)}, u32[]{:S(2)}) copy-start(s32[4,12]{1,0:T(4,128)} %param.4) | copy-start | bytes 580
  3.1 42.6 %collective-permute-start.1 = (bf16[4,256,512]{2,1,0:T(8,128)(2,1)S(1)}, bf16[4,256,512]{2,1,0:T(8,128)(2,1)S(1)}, u32[]{:S(2)}, u32[]{:S(2)}) collective-permute-start(bf16[4,256,512]{2,1,0:T(8,128)(2,1)S(1)} %bitcast.29), channel_id=1, source_target_pairs={{4,0},{8,4},{12,8},{16,12},{20,16},{24,20},{28,24},{32,28},{36,32}... | collective-permute-start | bytes 3145736 | tf_op jit(solution)/shard_map/ppermute | solution.py:21
  5.7 40.0 %collective-permute-start = (bf16[4,256,512]{2,1,0:T(8,128)(2,1)S(1)}, bf16[4,256,512]{2,1,0:T(8,128)(2,1)}, u32[]{:S(2)}, u32[]{:S(2)}) collective-permute-start(bf16[4,256,512]{2,1,0:T(8,128)(2,1)S(1)} %bitcast.30), channel_id=1, source_target_pairs={{0,4},{4,8},{8,12},{12,16},{16,20},{20,24},{24,28},{28,32},{32,36}... | collective-permute-start | bytes 3145736 | tf_op jit(solution)/shard_map/ppermute | solution.py:20
  8.7 55.9 %collective-permute-start.5 = (f32[4,256,128]{2,1,0:T(8,128)S(1)}, f32[4,256,128]{2,1,0:T(8,128)S(1)}, u32[]{:S(2)}, u32[]{:S(2)}) collective-permute-start(f32[4,256,128]{2,1,0:T(8,128)S(1)} %bitcast.23), channel_id=1, source_target_pairs={{4,0},{8,4},{12,8},{16,12},{20,16},{24,20},{28,24},{32,28},{36,32}... | collective-permute-start | bytes 1572872 | tf_op jit(solution)/shard_map/ppermute | solution.py:21
  11.3 53.4 %collective-permute-start.4 = (f32[4,256,128]{2,1,0:T(8,128)S(1)}, f32[4,256,128]{2,1,0:T(8,128)}, u32[]{:S(2)}, u32[]{:S(2)}) collective-permute-start(f32[4,256,128]{2,1,0:T(8,128)S(1)} %bitcast.24), channel_id=1, source_target_pairs={{0,4},{4,8},{8,12},{12,16},{16,20},{20,24},{24,28},{28,32},{32,36}... | collective-permute-start | bytes 1572872 | tf_op jit(solution)/shard_map/ppermute | solution.py:20
  56.6 9.2 %collective-permute-start.3 = (f32[4,256]{1,0:T(4,128)S(1)}, f32[4,256]{1,0:T(4,128)S(1)}, u32[]{:S(2)}, u32[]{:S(2)}) collective-permute-start(f32[4,256]{1,0:T(4,128)S(1)} %rsqrt.21), channel_id=1, source_target_pairs={{4,0},{8,4},{12,8},{16,12},{20,16},{24,20},{28,24},{32,28},{36,32}... | collective-permute-start | bytes 12296 | tf_op jit(solution)/shard_map/ppermute | solution.py:21
  62.5 7.6 %collective-permute-start.2 = (f32[4,256]{1,0:T(4,128)S(1)}, f32[4,256]{1,0:T(4,128)S(1)}, u32[]{:S(2)}, u32[]{:S(2)}) collective-permute-start(f32[4,256]{1,0:T(4,128)S(1)} %rsqrt.21), channel_id=1, source_target_pairs={{0,4},{4,8},{8,12},{12,16},{16,20},{20,24},{24,28},{28,32},{32,36}... | collective-permute-start | bytes 12296 | tf_op jit(solution)/shard_map/ppermute | solution.py:20
  372.4 10.5 %collective-permute-start.7 = (f32[4,256,128]{2,1,0:T(8,128)S(1)}, f32[4,256,128]{2,1,0:T(8,128)S(1)}, u32[]{:S(2)}, u32[]{:S(2)}) collective-permute-start(f32[4,256,128]{2,1,0:T(8,128)S(1)} %bitcast.26), channel_id=1, source_target_pairs={{4,0},{8,4},{12,8},{16,12},{20,16},{24,20},{28,24},{32,28},{36,32}... | collective-permute-start | bytes 1572872 | tf_op jit(solution)/shard_map/ppermute | solution.py:21
  377.3 8.0 %collective-permute-start.6 = (f32[4,256,128]{2,1,0:T(8,128)S(1)}, f32[4,256,128]{2,1,0:T(8,128)S(1)}, u32[]{:S(2)}, u32[]{:S(2)}) collective-permute-start(f32[4,256,128]{2,1,0:T(8,128)S(1)} %bitcast.27), channel_id=1, source_target_pairs={{0,4},{4,8},{8,12},{12,16},{16,20},{20,24},{24,28},{28,32},{32,36}... | collective-permute-start | bytes 1572872 | tf_op jit(solution)/shard_map/ppermute | solution.py:20
  563.8 10.5 %collective-permute-start.9 = (f32[4,256,128]{2,1,0:T(8,128)S(1)}, f32[4,256,128]{2,1,0:T(8,128)S(1)}, u32[]{:S(2)}, u32[]{:S(2)}) collective-permute-start(f32[4,256,128]{2,1,0:T(8,128)S(1)} %bitcast.33), channel_id=1, source_target_pairs={{4,0},{8,4},{12,8},{16,12},{20,16},{24,20},{28,24},{32,28},{36,32}... | collective-permute-start | bytes 1572872 | tf_op jit(solution)/shard_map/ppermute | solution.py:21
  568.7 8.0 %collective-permute-start.8 = (f32[4,256,128]{2,1,0:T(8,128)S(1)}, f32[4,256,128]{2,1,0:T(8,128)S(1)}, u32[]{:S(2)}, u32[]{:S(2)}) collective-permute-start(f32[4,256,128]{2,1,0:T(8,128)S(1)} %bitcast.34), channel_id=1, source_target_pairs={{0,4},{4,8},{8,12},{12,16},{16,20},{20,24},{24,28},{28,32},{32,36}... | collective-permute-start | bytes 1572872 | tf_op jit(solution)/shard_map/ppermute | solution.py:20
